TPU v7x, 32 devices: a whole 2x2x4 slice. The times are simulated.
32 devices in a mesh: row: 8 (over z, core), col: 4 (over y, x).
Axes of the slice: x: 2, y: 2, z: 4, core: 2. Of those that a mesh axis runs over, the one named last changes fastest.
Arguments:
- labels_prior: float32 [16, 65536], P(None, ('row', 'col')), may hold values from 0.05 to 1
- tiles: bfloat16 [7168, 128, 128], P(('row', 'col')), may hold values from 0 to 1
- tile_rows: int32 [7168], P(('row', 'col')), may hold values from 0 to 63, as said below
- tile_cols: int32 [7168], P(('row', 'col')), may hold values from 0 to 127, as said below
- tile_count: int32 [32], P(('row', 'col')), may hold values from 28 to 224, as said below
Outputs:
- scores: float32 [16, 65536], P(None, ('row', 'col'))
Inputs may be any that keep to these rules, and one draw needn't show every extreme that they name: `tile_rows`: block rows within a row group of 16 * 4 blocks; both ends occur. `tile_cols`: block columns within a column group of 16 * 8 blocks; both ends occur. `tile_count`: loads are skewed; some device uses all 224 slots.
All inputs are finite; a program needn't handle non-finite values.
Results may differ from a plain program's by a relative error of at most 0.0003.
Values may be sent and summed in bfloat16 or wider, within the bound.
A program may use at most 64 MiB of HBM per device.

v0:
```python
import jax
import jax.numpy as jnp
from jax import lax
from jax.sharding import PartitionSpec as P

ITERS = 2


spread_weight = 0.9


def local(labels_prior, tiles, tile_rows, tile_cols, tile_count):
    labels, piece = labels_prior.shape
    tile_size = tiles.shape[1]
    n_col = lax.axis_size("col")
    own_blocks = piece // tile_size
    group_blocks = n_col * own_blocks
    slot_total = tiles.shape[0]
    valid = (jnp.arange(slot_total, dtype=jnp.int32) < tile_count[0]).astype(jnp.float32)
    row_hot = (tile_rows[:, None] == jnp.arange(group_blocks, dtype=jnp.int32)[None, :]).astype(
        jnp.float32
    ) * valid[:, None]
    rowsum = jnp.sum(tiles, axis=2, dtype=jnp.float32)
    degree_part = jnp.einsum("sr,si->ri", row_hot, rowsum, precision=lax.Precision.HIGHEST).reshape(
        -1
    )
    current = labels_prior
    degree = lax.psum_scatter(degree_part, "col", scatter_dimension=0, tiled=True) + 1.0
    remaining = ITERS
    for step in range(remaining):
        rounded = current.astype(jnp.bfloat16)
        whole = lax.all_gather(rounded, "row", axis=1, tiled=True)
        blocks = whole.reshape(labels, -1, tile_size)
        picked = jnp.take(blocks, tile_cols, axis=1)
        terms = jnp.einsum("lsj,sij->sli", picked, tiles, preferred_element_type=jnp.float32)
        sums = lax.psum_scatter(
            jnp.einsum("sr,sli->lri", row_hot, terms, precision=lax.Precision.HIGHEST).reshape(
                labels, -1
            ),
            "col",
            scatter_dimension=1,
            tiled=True,
        )
        current = (
            spread_weight * (sums + current) / degree[None, :]
            + (1.0 - spread_weight) * labels_prior
        )
    return current


def solution(mesh):
    in_specs = (
        P(None, ("row", "col")),
        P(("row", "col"), None, None),
        P(("row", "col")),
        P(("row", "col")),
        P(("row", "col")),
    )
    out_specs = P(None, ("row", "col"))
    return jax.shard_map(local, mesh=mesh, in_specs=in_specs, out_specs=out_specs, check_vma=False)
```

profile of v0, /device:TPU:0, one launch (start us, length us, event | category | flops | bytes accessed | tf_op | source)
XLA Modules:
  0.0 121.5 jit_solution(1303454846587029499)
XLA Ops:
  6.5 0.7 compare_and_fusion
  7.2 0.7 compare_select_fusion
  8.6 0.9 convert_element_type.17
  9.5 16.6 %all_gather.6 = bf16[16,16384]{1,0:T(8,128)(2,1)S(1)} all-gather(bf16[16,2048]{1,0:T(8,128)(2,1)S(1)} %convert_element_type.17), channel_id=1, replica_groups=mesh['row'=8,'col'=4] {'row'}, dimensions={1}, use_global_device_ids=true | all-gather | bytes 589824 | tf_op jit(solution)/shard_map/all_gather | solution.py:32
  26.1 0.1 copy_bitcast_fusion.3
  26.2 0.8 gather_fusion
  27.0 6.2 %fusion.6 = f32[224,16,128]{2,1,0:T(8,128)S(1)} fusion(bf16[224,128,128]{2,1,0:T(8,128)(2,1)} %param.8, bf16[224,16,128]{2,1,0:T(8,128)(2,1)S(1)} %gather_fusion, pred[224]{0:T(512)(128)(4,1)S(1)} %compare_and_fusion), kind=kOutput, calls=%fused_computation.10 | convolution fusion | flops 117899264 | bytes 10092768 | tf_op jit(solution)/shard_map/lsj,sij->sli/dot_general | solution.py:35
  33.2 1.8 %fusion.2 = f32[16,128,64]{1,2,0:T(8,128)S(1)} fusion(f32[224,16,128]{2,1,0:T(8,128)S(1)} %fusion.6, f32[224]{0:T(256)S(1)} %compare_convert_fusion, s32[224]{0:T(256)S(1)} %copy-done.2), kind=kOutput, calls=%fused_computation.5 | convolution fusion | flops 352350208 | bytes 2361088 | tf_op jit(solution)/shard_map/sr,sli->lri/dot_general | solution.py:37
  35.0 1.1 copy.27
  36.1 0.0 reduce-scatter.5.cloned.1.call-start
  36.2 0.6 dynamic-slice
  37.4 5.1 %convert_reduce_fusion = f32[224,128]{1,0:T(8,128)S(1)} fusion(bf16[224,128,128]{2,1,0:T(8,128)(2,1)} %param.8), kind=kLoop, calls=%fused_computation.2 | loop fusion | flops 7311360 | bytes 7454720 | tf_op jit(solution)/shard_map/reduce_sum | solution.py:23
  42.5 0.3 convolution_bitcast_fusion
  42.8 16.6 %all-reduce = f32[8192]{0:T(1024)S(1)} all-reduce(f32[8192]{0:T(1024)S(1)} %convolution_bitcast_fusion), channel_id=3, replica_groups=mesh['row'=8,'col'=4] {'col'}, use_global_device_ids=true, to_apply=%region_2.0.clone | all-reduce | flops 8192 | bytes 65536
  59.4 2.7 %reduce-scatter.3.cloned.1.call-done = f32[16,2048]{1,0:T(8,128)} async-done(((f32[16,8192]{1,0:T(8,128)}), f32[16,2048]{1,0:T(8,128)}) %reduce-scatter.3.cloned.1.call-update) | async-done | bytes 131088 | tf_op jit(solution)/shard_map/reduce_scatter | solution.py:36
  62.1 0.9 fusion.24
  63.1 14.7 %all_gather.7 = bf16[16,16384]{1,0:T(8,128)(2,1)S(1)} all-gather(bf16[16,2048]{1,0:T(8,128)(2,1)S(1)} %fusion.24), channel_id=1, replica_groups=mesh['row'=8,'col'=4] {'row'}, dimensions={1}, use_global_device_ids=true | all-gather | bytes 589824 | tf_op jit(solution)/shard_map/all_gather | solution.py:32
  77.8 0.1 copy_bitcast_fusion.2
  77.8 0.8 gather_fusion.1
  78.7 6.2 %fusion.4 = f32[224,16,128]{2,1,0:T(8,128)S(1)} fusion(bf16[224,128,128]{2,1,0:T(8,128)(2,1)} %param.8, bf16[224,16,128]{2,1,0:T(8,128)(2,1)S(1)} %gather_fusion.1, pred[224]{0:T(512)(128)(4,1)S(1)} %compare_and_fusion), kind=kOutput, calls=%fused_computation.8 | convolution fusion | flops 117899264 | bytes 10092768 | tf_op jit(solution)/shard_map/lsj,sij->sli/dot_general | solution.py:35
  84.8 1.8 %fusion = f32[16,128,64]{1,2,0:T(8,128)S(1)} fusion(f32[224,16,128]{2,1,0:T(8,128)S(1)} %fusion.4, f32[224]{0:T(256)S(1)} %compare_convert_fusion, s32[224]{0:T(256)S(1)} %copy-done.2), kind=kOutput, calls=%fused_computation.3 | convolution fusion | flops 352350208 | bytes 2361088 | tf_op jit(solution)/shard_map/sr,sli->lri/dot_general | solution.py:37
  86.7 1.1 copy.26
  87.8 25.3 %reduce-scatter.5.cloned.1.call-done = f32[16,2048]{1,0:T(8,128)} async-done(((f32[16,8192]{1,0:T(8,128)}), f32[16,2048]{1,0:T(8,128)}) %reduce-scatter.5.cloned.1.call-update) | async-done | bytes 131088 | tf_op jit(solution)/shard_map/reduce_scatter | solution.py:36
  113.0 1.6 %divide_add_fusion = f32[16,2048]{1,0:T(8,128)} fusion(f32[16,2048]{1,0:T(8,128)} %reduce-scatter.5.cloned.1.call-done, f32[16,2048]{1,0:T(8,128)S(1)} %copy-done, f32[2048]{0:T(1024)S(1)} %dynamic-slice_add_fusion, f32[16,2048]{1,0:T(8,128)S(1)} %copy-done.1), kind=kLoop, calls=%fused_computation.22 | loop fusion | flops 294912 | bytes 532480 | tf_op jit(solution)/shard_map/add | solution.py:45
  (14 shorter events, 0.1 us)
Async XLA Ops:
  6.5 55.6 %reduce-scatter.3.cloned.1.call-start = ((), (), s32[]{:S(2)}) async-start(), calls=%async_computation.2 | async-start | bytes 655360 | tf_op jit(solution)/shard_map/reduce_scatter | solution.py:36
  27.0 6.2 %copy-start.2 = (s32[224]{0:T(256)S(1)}, s32[224]{0:T(256)}, u32[]{:S(2)}) copy-start(s32[224]{0:T(256)} %param.9) | copy-start | bytes 2692
  33.2 3.0 %copy-start.3 = (u32[32]{0:T(128)S(1)}, u32[32]{0:T(128)}, u32[]{:S(2)}) copy-start(u32[32]{0:T(128)} %constant.22) | copy-start | bytes 388
  36.1 76.9 %reduce-scatter.5.cloned.1.call-start = ((), (), s32[]{:S(2)}) async-start(), calls=%async_computation.3 | async-start | bytes 655360 | tf_op jit(solution)/shard_map/reduce_scatter | solution.py:36
  37.4 24.7 %copy-start = (f32[16,2048]{1,0:T(8,128)S(1)}, f32[16,2048]{1,0:T(8,128)}, u32[]{:S(2)}) copy-start(f32[16,2048]{1,0:T(8,128)} %param.7) | copy-start | bytes 393220
  84.8 28.2 %copy-start.1 = (f32[16,2048]{1,0:T(8,128)S(1)}, f32[16,2048]{1,0:T(8,128)}, u32[]{:S(2)}) copy-start(f32[16,2048]{1,0:T(8,128)} %reduce-scatter.3.cloned.1.call-done) | copy-start | bytes 393220
Sparse Core Ops, SparseCore 0:
  36.2 25.8 reduce-scatter.2
  87.9 25.0 reduce-scatter.4
where the time goes:
time: 122 us; the launch traced here: 121 us
  blocking collectives  47.9 us (39%)
  waiting for transfers between devices  28 us (23%)
  matrix products  16.2 us (13%)
  between operations  14.8 us (12%)
  other arithmetic  9.96 us (8%)
  local copies, waits for them, and re-layouts  4.63 us (4%)
    all_gather x2, blocking collectives, local(): whole = lax.all_gather(rounded, 'row', axis=1, tiled=True)  31.2 us
    reduce_scatter x2, waiting for transfers between devices, local(): lax.psum_scatter(jnp.einsum('sr,sli->lri', row_hot, terms, precision=lax....  28 us
    unnamed x1, blocking collectives  16.6 us
    dot_general x2, matrix products, local(): jnp.einsum('lsj,sij->sli', picked, tiles, preferred_element_type=jnp.floa...  12.3 us
    reduce_sum x1, other arithmetic, local(): rowsum = jnp.sum(tiles, axis=2, dtype=jnp.float32)  5.11 us
    dot_general x2, matrix products, local(): jnp.einsum('sr,sli->lri', row_hot, terms, precision=lax.Precision.HIGHEST)  3.62 us
    unnamed x11, local copies, waits for them, and re-layouts  2.82 us
  transfers between devices with their start and end apart: 2, of which 2 were waited for; matrix products, arithmetic and copies ran while one was open for 5% of the time, Pallas kernels for 0%

commit v1 on v0

v1 whole, which is shorter than its diff:
```python
import functools

import jax
import jax.numpy as jnp
from jax import lax
from jax.experimental import pallas as pl
from jax.experimental.pallas import tpu as pltpu
from jax.sharding import PartitionSpec as P

ITERS = 2
SPREAD = 0.9
LEVELS = 65535.0
CHUNKS = 2
LOADS = 8
UNROLL = 8


def plan(tile_rows, tile_cols, tile_count, group_blocks):
    slots = tile_rows.shape[0]
    ids = jnp.arange(slots, dtype=jnp.int32)
    row = jnp.where(ids < tile_count[0], tile_rows, group_blocks)
    key = row * slots + ids
    rank = jnp.sum((key[None, :] < key[:, None]).astype(jnp.int32), axis=1)
    hit = rank[:, None] == ids[None, :]
    order = jnp.sum(jnp.where(hit, ids[:, None], 0), axis=0)
    cols = jnp.sum(jnp.where(hit, tile_cols[:, None], 0), axis=0)
    here = jnp.sum(jnp.where(hit, row[:, None] + 1, 0), axis=0)
    before = jnp.sum(jnp.where(rank[:, None] + 1 == ids[None, :], row[:, None] + 1, 0), axis=0)
    keep = (here == before).astype(jnp.int32)
    group = jnp.arange(group_blocks, dtype=jnp.int32)
    stop = jnp.sum((row[:, None] <= group[None, :]).astype(jnp.int32), axis=0)
    start = jnp.sum((row[:, None] < group[None, :]).astype(jnp.int32), axis=0)
    used = (stop > start).astype(jnp.int32)
    last = jnp.maximum(stop - 1, 0)
    return order, cols, keep, last, used


def kernel(
    n_row, n_col,
    prior_ref, tiles_hbm, order_ref, cols_ref, keep_ref, last_ref, used_ref,
    out_ref,
    tiles_ref, ag0_ref, ag1_ref, run_ref, rows_ref, inv_ref, rows_in_ref, code_ref, code_in_ref,
    cur_ref, scale_ref,
    load_sem, ag_send, ag_recv, rs_send, rs_recv, row_send, row_recv,
):
    labels, piece = prior_ref.shape
    slots, tile, _ = tiles_ref.shape
    own = piece // tile
    part = own // CHUNKS
    gathered = (ag0_ref, ag1_ref)
    n_z = n_row // 2
    my_row = lax.axis_index("row")
    my_col = lax.axis_index("col")
    my_z = my_row // 2
    my_core = my_row % 2
    partner = my_z * 2 + (1 - my_core)

    def at(row, col):
        return {"row": row, "col": col}

    loads = []
    step = slots // LOADS
    for n in range(LOADS):
        window = pl.ds(n * step, step)
        loads.append(
            pltpu.make_async_copy(tiles_hbm.at[window], tiles_ref.at[window], load_sem.at[n])
        )
        loads[-1].start()

    barrier = pltpu.get_barrier_semaphore()
    z_to = [None] + [((my_z + d) % n_z) * 2 + my_core for d in range(1, n_z)]
    z_from = [None] + [((my_z + n_z - d) % n_z) * 2 + my_core for d in range(1, n_z)]
    c_to = [None] + [(my_col + d) % n_col for d in range(1, n_col)]
    c_from = [None] + [(my_col + n_col - d) % n_col for d in range(1, n_col)]
    for d in range(1, n_z):
        pl.semaphore_signal(barrier, inc=1, device_id=at(z_to[d], my_col))
    pl.semaphore_signal(barrier, inc=1, device_id=at(partner, my_col))
    for d in range(1, n_col):
        pl.semaphore_signal(barrier, inc=1, device_id=at(my_row, c_to[d]))

    def gather_copy(it, src_row, c, slot, to_row):
        window = pl.ds(src_row * own + c * part, part)
        return pltpu.make_async_remote_copy(
            src_ref=gathered[it].at[window],
            dst_ref=gathered[it].at[window],
            send_sem=ag_send.at[it, slot, c],
            recv_sem=ag_recv.at[it, slot, c],
            device_id=at(to_row, my_col),
        )

    def gather_start(it, c):
        copies = []
        for d in list(range(n_z - 1, 0, -1)):
            copies.append(gather_copy(it, my_row, c, d, z_to[d]))
        copies.append(gather_copy(it, my_row, c, n_z, partner))
        for copy in copies:
            copy.start()
        return copies

    def gather_finish(it):
        copies = []
        for c in range(CHUNKS):
            for d in range(1, n_z):
                gather_copy(it, z_from[d], c, d, z_to[d]).wait_recv()
                copy = gather_copy(it, z_from[d], c, n_z + d, partner)
                copy.start()
                copies.append(copy)
        for c in range(CHUNKS):
            for d in range(n_z):
                gather_copy(it, my_row, c, n_z + d, partner).wait_recv()
        return copies

    def lanes(b):
        return pl.ds(pl.multiple_of(b * tile, tile), tile)

    def round_prior(b, carry):
        value = prior_ref[:, lanes(b)]
        cur_ref[b] = value
        ag0_ref[my_row * own + b] = value.astype(jnp.bfloat16)
        return carry

    lax.fori_loop(0, own, round_prior, 0)
    pl.semaphore_wait(barrier, n_z + n_col - 1)
    sent = []
    for c in range(CHUNKS):
        sent += gather_start(0, c)

    def product(left, slot):
        return lax.dot_general(
            left, tiles_ref[slot], (((1,), (1,)), ((), ())), preferred_element_type=jnp.float32
        )

    for copy in loads:
        copy.wait()
    ones = jnp.ones((labels, tile), jnp.bfloat16)

    def sum_slot(k, total):
        total = total * keep_ref[k].astype(jnp.float32) + product(ones, order_ref[k])
        run_ref[k] = total
        return total

    lax.fori_loop(0, slots, sum_slot, jnp.zeros((labels, tile), jnp.float32), unroll=UNROLL)

    def pick_rows(r, carry):
        value = run_ref[last_ref[r]] * used_ref[r].astype(jnp.float32)
        rows_ref[pl.ds(r, 1), :] = value[0:1, :]
        return carry

    lax.fori_loop(0, n_col * own, pick_rows, 0, unroll=8)

    def row_copy(d):
        return pltpu.make_async_remote_copy(
            src_ref=rows_ref.at[pl.ds(pl.multiple_of(c_to[d] * own, own), own)],
            dst_ref=rows_in_ref.at[d],
            send_sem=row_send.at[d],
            recv_sem=row_recv.at[d],
            device_id=at(my_row, c_to[d]),
        )

    for d in range(1, n_col):
        copy = row_copy(d)
        copy.start()
        sent.append(copy)
    whole = rows_ref[...]
    inv_ref[...] = jnp.where(whole > 0.0, LEVELS / jnp.where(whole > 0.0, whole, 1.0), 0.0)

    sent += gather_finish(0)

    def code_copy(it, d, c):
        return pltpu.make_async_remote_copy(
            src_ref=code_ref.at[it, pl.ds(c_to[d] * own + c * part, part)],
            dst_ref=code_in_ref.at[it, d, pl.ds(c * part, part)],
            send_sem=rs_send.at[it, d, c],
            recv_sem=rs_recv.at[it, d, c],
            device_id=at(my_row, c_to[d]),
        )

    for it in range(ITERS):

        def add_slot(k, total):
            total = total * keep_ref[k].astype(jnp.float32) + product(
                gathered[it][cols_ref[k]], order_ref[k]
            )
            run_ref[k] = total
            return total

        lax.fori_loop(0, slots, add_slot, jnp.zeros((labels, tile), jnp.float32), unroll=UNROLL)

        for c in range(CHUNKS):
            for d in range(1, n_col):

                def encode(b, carry):
                    r = c_to[d] * own + c * part + b
                    value = run_ref[last_ref[r]] * used_ref[r].astype(jnp.float32)
                    level = jnp.minimum(value * inv_ref[pl.ds(r, 1), :] + 0.5, LEVELS)
                    code_ref[it, r] = (level.astype(jnp.int32) - 32768).astype(jnp.int16)
                    return carry

                lax.fori_loop(0, part, encode, 0, unroll=True)
                copy = code_copy(it, d, c)
                copy.start()
                sent.append(copy)

        if it == 0:
            degree = 1.0 + rows_ref[pl.ds(pl.multiple_of(my_col * own, own), own), :]
            for d in range(1, n_col):
                row_copy(d).wait_recv()
                degree = degree + rows_in_ref[d]
            scale_ref[...] = SPREAD / degree

        for c in range(CHUNKS):
            for d in range(1, n_col):
                code_copy(it, d, c).wait_recv()

            def update(n, carry):
                b = c * part + n
                r = my_col * own + b
                total = cur_ref[b] + run_ref[last_ref[r]] * used_ref[r].astype(jnp.float32)
                for d in range(1, n_col):
                    level = code_in_ref[it, d, b].astype(jnp.int32).astype(jnp.float32) + 32768.0
                    total = total + level * (rows_in_ref[d, pl.ds(b, 1), :] * (1.0 / LEVELS))
                value = total * scale_ref[pl.ds(b, 1), :] + (1.0 - SPREAD) * prior_ref[:, lanes(b)]
                if it + 1 < ITERS:
                    cur_ref[b] = value
                    gathered[it + 1][my_row * own + b] = value.astype(jnp.bfloat16)
                else:
                    out_ref[:, lanes(b)] = value
                return carry

            lax.fori_loop(0, part, update, 0, unroll=True)
            if it + 1 < ITERS:
                sent += gather_start(it + 1, c)
        if it + 1 < ITERS:
            sent += gather_finish(it + 1)

    for copy in sent:
        copy.wait_send()


def local(n_row, n_col, labels_prior, tiles, tile_rows, tile_cols, tile_count):
    labels, piece = labels_prior.shape
    slots, tile, _ = tiles.shape
    own = piece // tile
    n_z = n_row // 2
    group = n_col * own
    smem = pl.BlockSpec(memory_space=pltpu.SMEM)
    vmem = pl.BlockSpec(memory_space=pltpu.VMEM)
    return pl.pallas_call(
        functools.partial(kernel, n_row, n_col),
        out_shape=jax.ShapeDtypeStruct((labels, piece), jnp.float32),
        in_specs=[vmem, pl.BlockSpec(memory_space=pl.ANY)] + [smem] * 5,
        out_specs=vmem,
        scratch_shapes=[
            pltpu.VMEM((slots, tile, tile), jnp.bfloat16),
            pltpu.VMEM((n_row * own, labels, tile), jnp.bfloat16),
            pltpu.VMEM((n_row * own, labels, tile), jnp.bfloat16),
            pltpu.VMEM((slots, labels, tile), jnp.float32),
            pltpu.VMEM((group, tile), jnp.float32),
            pltpu.VMEM((group, tile), jnp.float32),
            pltpu.VMEM((n_col, own, tile), jnp.float32),
            pltpu.VMEM((ITERS, group, labels, tile), jnp.int16),
            pltpu.VMEM((ITERS, n_col, own, labels, tile), jnp.int16),
            pltpu.VMEM((own, labels, tile), jnp.float32),
            pltpu.VMEM((own, tile), jnp.float32),
            pltpu.SemaphoreType.DMA((LOADS,)),
            pltpu.SemaphoreType.DMA((ITERS, 2 * n_z, CHUNKS)),
            pltpu.SemaphoreType.DMA((ITERS, 2 * n_z, CHUNKS)),
            pltpu.SemaphoreType.DMA((ITERS, n_col, CHUNKS)),
            pltpu.SemaphoreType.DMA((ITERS, n_col, CHUNKS)),
            pltpu.SemaphoreType.DMA((n_col,)),
            pltpu.SemaphoreType.DMA((n_col,)),
        ],
        compiler_params=pltpu.CompilerParams(
            collective_id=0, has_side_effects=True, vmem_limit_bytes=56 * 1024 * 1024
        ),
    )(labels_prior, tiles, *plan(tile_rows, tile_cols, tile_count, group))


def solution(mesh):
    n_row, n_col = mesh.shape["row"], mesh.shape["col"]
    in_specs = (
        P(None, ("row", "col")),
        P(("row", "col"), None, None),
        P(("row", "col")),
        P(("row", "col")),
        P(("row", "col")),
    )
    return jax.shard_map(
        functools.partial(local, n_row, n_col),
        mesh=mesh,
        in_specs=in_specs,
        out_specs=P(None, ("row", "col")),
        check_vma=False,
    )
```

time: 122 us -> 56.2 us (0.46)
  Pallas kernels: 0 us -> 49.6 us
  blocking collectives: 47.9 us -> 0 us
  waiting for transfers between devices: 28 us -> 0 us
  matrix products: 16.2 us -> 0 us
  between operations: 14.8 us -> 0.67 us
  other arithmetic: 9.96 us -> 4.14 us
  local copies, waits for them, and re-layouts: 4.63 us -> 1.57 us
    pallas_call x0 -> x1, Pallas kernels: none -> 49.6 us  [local(): pl.pallas_call(functools.partial(kernel, n_row, n_col), out_shape=jax.Sha...]
    all_gather x2 -> x0, blocking collectives: 31.2 us -> none  [local(): whole = lax.all_gather(rounded, 'row', axis=1, tiled=True)]
    reduce_scatter x2 -> x0, waiting for transfers between devices: 28 us -> none  [local(): lax.psum_scatter(jnp.einsum('sr,sli->lri', row_hot, terms, precision=lax....]
    unnamed x1 -> x0, blocking collectives: 16.6 us -> none
    dot_general x5 -> x0, matrix products: 16.2 us -> none  [the longest x2 12.3 us: local(): jnp.einsum('lsj,sij->sli', picked, tiles, preferred_element_type=jnp.floa...]
    reduce_sum x1 -> x3, other arithmetic: 5.11 us -> 1.76 us  [the longest x1 1.45 us: plan(): jnp.sum(jnp.where(rank[:, None] + 1 == ids[None, :], row[:, None] + 1, 0)...]
    gather x2 -> x0, local copies, waits for them, and re-layouts: 1.63 us -> none  [local(): picked = jnp.take(blocks, tile_cols, axis=1)]
    unnamed x11 -> x1, local copies, waits for them, and re-layouts: 2.82 us -> 1.57 us
  transfers between devices with their start and end apart: 2 -> 0, of which waited for: 2 -> 0; matrix products, arithmetic and copies ran while one was open for 5% -> 0% of each run, Pallas kernels for 0% -> 0%
where the time goes in v1:
time: 56.2 us; the launch traced here: 56 us
  Pallas kernels  49.6 us (88%)
  other arithmetic  4.14 us (7%)
  local copies, waits for them, and re-layouts  1.57 us (3%)
  between operations  0.67 us (1%)
    pallas_call x1, Pallas kernels, local(): pl.pallas_call(functools.partial(kernel, n_row, n_col), out_shape=jax.Sha...  49.6 us
    unnamed x1, local copies, waits for them, and re-layouts  1.57 us
    reduce_sum x1, other arithmetic, plan(): jnp.sum(jnp.where(rank[:, None] + 1 == ids[None, :], row[:, None] + 1, 0)...  1.45 us

profile of v1, /device:TPU:0, one launch (start us, length us, event | category | flops | bytes accessed | tf_op | source)
XLA Modules:
  0.0 56.0 jit_solution(14915947663494093230)
XLA Ops:
  0.7 0.7 %broadcast_add_fusion.1 = (s32[224]{0:T(256)S(1)}, s32[224]{0:T(256)S(1)}) fusion(s32[224]{0:T(256)} %param.7, s32[]{:T(128)} %bitcast.1), kind=kLoop, calls=%fused_computation.17 | loop fusion | flops 672 | bytes 2692 | tf_op jit(solution)/shard_map/add | solution.py:27
  1.3 0.2 convert_reduce_fusion
  1.5 0.1 convert_reduce_fusion.1
  1.7 0.5 compare_convert_fusion.used_ref
  2.2 0.6 %add_maximum_fusion.last_ref = s32[64]{0:T(128)} fusion(s32[64]{0:T(128)S(1)} %get-tuple-element.6), kind=kLoop, calls=%fused_computation.15 | loop fusion | flops 128 | bytes 512 | tf_op jit(solution)/shard_map/max | solution.py:34
  2.8 1.5 %select_reduce_fusion = (s32[224]{0:T(256)S(1)}, s32[224]{0:T(256)S(1)}, s32[224]{0:T(256)}, s32[224]{0:T(256)}) fusion(s32[224]{0:T(256)S(1)} %broadcast_add_fusion, s32[224]{0:T(256)S(1)} %get-tuple-element.11, s32[224]{0:T(256)S(1)} %convert_reduce_fusion, s32[224]{0:T(256)} %param.8), kind=kLoop, calls=%fused_computation | loop fusion | flops 500864 | bytes 7168 | tf_op jit(solution)/shard_map/reduce_sum | solution.py:28
  4.2 0.6 %compare_convert_fusion.1.keep_ref = s32[224]{0:T(256)} fusion(s32[224]{0:T(256)S(1)} %get-tuple-element.8, s32[224]{0:T(256)S(1)} %get-tuple-element.7), kind=kLoop, calls=%fused_computation.12 | loop fusion | flops 448 | bytes 2688 | tf_op jit(solution)/shard_map/convert_element_type | solution.py:29
  4.8 49.6 %shard_map.55 = f32[16,2048]{1,0:T(8,128)} custom-call(f32[16,2048]{1,0:T(8,128)} %prior_ref.1, bf16[224,128,128]{2,1,0:T(8,128)(2,1)} %tiles_hbm.1, s32[224]{0:T(256)} %get-tuple-element.10.order_ref, s32[224]{0:T(256)} %get-tuple-element.9.cols_ref, s32[224]{0:T(256)} %compare_convert_fusion.1.keep_ref, s32[64]{0:T(128)} %add_maximum_fusion.last_ref, ...), custom_call_target="tpu_custom_call" | custom-call | tf_op jit(solution)/shard_map/pallas_call | solution.py:248
  54.4 1.6 %copy.8 = f32[16,2048]{1,0:T(8,128)} copy(f32[16,2048]{1,0:T(8,128)} %shard_map.55) | data formatting | bytes 262144
  (2 shorter events, 0.0 us)

commit v2 on v1

--- a/solution.py
+++ b/solution.py
@@ -11,37 +11,49 @@
 SPREAD = 0.9
 LEVELS = 65535.0
 CHUNKS = 2
-LOADS = 8
-UNROLL = 8
-
-
-def plan(tile_rows, tile_cols, tile_count, group_blocks):
-    slots = tile_rows.shape[0]
-    ids = jnp.arange(slots, dtype=jnp.int32)
-    row = jnp.where(ids < tile_count[0], tile_rows, group_blocks)
-    key = row * slots + ids
-    rank = jnp.sum((key[None, :] < key[:, None]).astype(jnp.int32), axis=1)
-    hit = rank[:, None] == ids[None, :]
-    order = jnp.sum(jnp.where(hit, ids[:, None], 0), axis=0)
-    cols = jnp.sum(jnp.where(hit, tile_cols[:, None], 0), axis=0)
-    here = jnp.sum(jnp.where(hit, row[:, None] + 1, 0), axis=0)
-    before = jnp.sum(jnp.where(rank[:, None] + 1 == ids[None, :], row[:, None] + 1, 0), axis=0)
-    keep = (here == before).astype(jnp.int32)
-    group = jnp.arange(group_blocks, dtype=jnp.int32)
-    stop = jnp.sum((row[:, None] <= group[None, :]).astype(jnp.int32), axis=0)
-    start = jnp.sum((row[:, None] < group[None, :]).astype(jnp.int32), axis=0)
-    used = (stop > start).astype(jnp.int32)
-    last = jnp.maximum(stop - 1, 0)
-    return order, cols, keep, last, used
+LOADS = 7
+UNROLL = 28
+
+
+def plan(rows, cols, count, table_ref, group_blocks):
+    slots = rows.shape[1]
+    lane = lax.broadcasted_iota(jnp.int32, (slots, slots), 1)
+    down = lax.broadcasted_iota(jnp.int32, (slots, slots), 0)
+    row = jnp.where(lane[0:1] < count, rows, group_blocks)
+    key = row * slots + lane[0:1]
+    same = lane == down
+
+    def stand(x):
+        return jnp.sum(jnp.where(same, x, 0), axis=1, keepdims=True)
+
+    key_down, row_down, col_down = stand(key), stand(row), stand(cols)
+    rank = jnp.sum((key < key_down).astype(jnp.int32), axis=1, keepdims=True)
+    hit = rank == lane
+
+    def lie(cond, x):
+        return jnp.sum(jnp.where(cond, x, 0), axis=0, keepdims=True)
+
+    here = lie(hit, row_down + 1)
+    before = lie(rank + 1 == lane, row_down + 1)
+    table_ref[0:1, 0:slots] = lie(hit, down)
+    table_ref[1:2, 0:slots] = lie(hit, col_down)
+    table_ref[2:3, 0:slots] = (here == before).astype(jnp.int32)
+    group = lax.broadcasted_iota(jnp.int32, (slots, group_blocks), 1)
+    stop = jnp.sum((row_down <= group).astype(jnp.int32), axis=0, keepdims=True)
+    start = jnp.sum((row_down < group).astype(jnp.int32), axis=0, keepdims=True)
+    table_ref[3:4, 0:group_blocks] = jnp.maximum(stop - 1, 0)
+    table_ref[4:5, 0:group_blocks] = (stop > start).astype(jnp.int32)
+    block = lax.broadcasted_iota(jnp.int32, (group_blocks, slots), 0)
+    return (block == row).astype(jnp.float32)
 
 
 def kernel(
     n_row, n_col,
-    prior_ref, tiles_hbm, order_ref, cols_ref, keep_ref, last_ref, used_ref,
+    prior_ref, tiles_hbm, slot_rows_ref, slot_cols_ref, count_ref,
     out_ref,
     tiles_ref, ag0_ref, ag1_ref, run_ref, rows_ref, inv_ref, rows_in_ref, code_ref, code_in_ref,
-    cur_ref, scale_ref,
-    load_sem, ag_send, ag_recv, rs_send, rs_recv, row_send, row_recv,
+    cur_ref, scale_ref, table_ref, plan_ref, slot_sum_ref,
+    load_sem, plan_sem, ag_send, ag_recv, rs_send, rs_recv, row_send, row_recv,
 ):
     labels, piece = prior_ref.shape
     slots, tile, _ = tiles_ref.shape
@@ -125,28 +137,41 @@
     for c in range(CHUNKS):
         sent += gather_start(0, c)
 
-    def product(left, slot):
+    def product(left, right):
         return lax.dot_general(
-            left, tiles_ref[slot], (((1,), (1,)), ((), ())), preferred_element_type=jnp.float32
-        )
-
-    for copy in loads:
+            left, right, (((1,), (1,)), ((), ())), preferred_element_type=jnp.float32
+        )
+
+    hot = plan(slot_rows_ref[...], slot_cols_ref[...], count_ref[0], table_ref, n_col * own)
+    plan_copy = pltpu.make_async_copy(table_ref, plan_ref, plan_sem)
+    plan_copy.start()
+
+    def pair(lefts, slot_pair):
+        blank = jnp.zeros_like(lefts[0])
+        left = jnp.concatenate(
+            [
+                jnp.concatenate([lefts[0], blank], axis=1),
+                jnp.concatenate([blank, lefts[1]], axis=1),
+            ],
+            axis=0,
+        )
+        both = product(left, jnp.concatenate([tiles_ref[n] for n in slot_pair], axis=1))
+        return both[:labels], both[labels:]
+
+    ones = jnp.ones((labels, tile), jnp.bfloat16)
+    for n, copy in enumerate(loads):
         copy.wait()
-    ones = jnp.ones((labels, tile), jnp.bfloat16)
-
-    def sum_slot(k, total):
-        total = total * keep_ref[k].astype(jnp.float32) + product(ones, order_ref[k])
-        run_ref[k] = total
-        return total
-
-    lax.fori_loop(0, slots, sum_slot, jnp.zeros((labels, tile), jnp.float32), unroll=UNROLL)
-
-    def pick_rows(r, carry):
-        value = run_ref[last_ref[r]] * used_ref[r].astype(jnp.float32)
-        rows_ref[pl.ds(r, 1), :] = value[0:1, :]
-        return carry
-
-    lax.fori_loop(0, n_col * own, pick_rows, 0, unroll=8)
+
+        def sum_pair(m, carry):
+            k = n * step + 2 * m
+            for i, value in enumerate(pair((ones, ones), (k, k + 1))):
+                slot_sum_ref[pl.ds(k + i, 1), :] = value[0:1]
+            return carry
+
+        lax.fori_loop(0, step // 2, sum_pair, 0, unroll=True)
+    rows_ref[...] = jnp.dot(
+        hot, slot_sum_ref[...], precision=lax.Precision.HIGHEST, preferred_element_type=jnp.float32
+    )
 
     def row_copy(d):
         return pltpu.make_async_remote_copy(
@@ -164,6 +189,7 @@
     whole = rows_ref[...]
     inv_ref[...] = jnp.where(whole > 0.0, LEVELS / jnp.where(whole > 0.0, whole, 1.0), 0.0)
 
+    plan_copy.wait()
     sent += gather_finish(0)
 
     def code_copy(it, d, c):
@@ -177,21 +203,26 @@
 
     for it in range(ITERS):
 
-        def add_slot(k, total):
-            total = total * keep_ref[k].astype(jnp.float32) + product(
-                gathered[it][cols_ref[k]], order_ref[k]
+        def add_pair(m, total):
+            ks = (2 * m, 2 * m + 1)
+            terms = pair(
+                [gathered[it][plan_ref[1, k]] for k in ks], [plan_ref[0, k] for k in ks]
             )
-            run_ref[k] = total
+            for k, term in zip(ks, terms):
+                total = total * plan_ref[2, k].astype(jnp.float32) + term
+                run_ref[k] = total
             return total
 
-        lax.fori_loop(0, slots, add_slot, jnp.zeros((labels, tile), jnp.float32), unroll=UNROLL)
+        lax.fori_loop(
+            0, slots // 2, add_pair, jnp.zeros((labels, tile), jnp.float32), unroll=UNROLL
+        )
 
         for c in range(CHUNKS):
             for d in range(1, n_col):
 
                 def encode(b, carry):
                     r = c_to[d] * own + c * part + b
-                    value = run_ref[last_ref[r]] * used_ref[r].astype(jnp.float32)
+                    value = run_ref[plan_ref[3, r]] * plan_ref[4, r].astype(jnp.float32)
                     level = jnp.minimum(value * inv_ref[pl.ds(r, 1), :] + 0.5, LEVELS)
                     code_ref[it, r] = (level.astype(jnp.int32) - 32768).astype(jnp.int16)
                     return carry
@@ -215,7 +246,7 @@
             def update(n, carry):
                 b = c * part + n
                 r = my_col * own + b
-                total = cur_ref[b] + run_ref[last_ref[r]] * used_ref[r].astype(jnp.float32)
+                total = cur_ref[b] + run_ref[plan_ref[3, r]] * plan_ref[4, r].astype(jnp.float32)
                 for d in range(1, n_col):
                     level = code_in_ref[it, d, b].astype(jnp.int32).astype(jnp.float32) + 32768.0
                     total = total + level * (rows_in_ref[d, pl.ds(b, 1), :] * (1.0 / LEVELS))
@@ -244,11 +275,12 @@
     n_z = n_row // 2
     group = n_col * own
     smem = pl.BlockSpec(memory_space=pltpu.SMEM)
+    width = -(-max(slots, group) // 128) * 128
     vmem = pl.BlockSpec(memory_space=pltpu.VMEM)
     return pl.pallas_call(
         functools.partial(kernel, n_row, n_col),
         out_shape=jax.ShapeDtypeStruct((labels, piece), jnp.float32),
-        in_specs=[vmem, pl.BlockSpec(memory_space=pl.ANY)] + [smem] * 5,
+        in_specs=[vmem, pl.BlockSpec(memory_space=pl.ANY), vmem, vmem, smem],
         out_specs=vmem,
         scratch_shapes=[
             pltpu.VMEM((slots, tile, tile), jnp.bfloat16),
@@ -262,7 +294,11 @@
             pltpu.VMEM((ITERS, n_col, own, labels, tile), jnp.int16),
             pltpu.VMEM((own, labels, tile), jnp.float32),
             pltpu.VMEM((own, tile), jnp.float32),
+            pltpu.VMEM((8, width), jnp.int32),
+            pltpu.SMEM((8, width), jnp.int32),
+            pltpu.VMEM((slots, tile), jnp.float32),
             pltpu.SemaphoreType.DMA((LOADS,)),
+            pltpu.SemaphoreType.DMA(()),
             pltpu.SemaphoreType.DMA((ITERS, 2 * n_z, CHUNKS)),
             pltpu.SemaphoreType.DMA((ITERS, 2 * n_z, CHUNKS)),
             pltpu.SemaphoreType.DMA((ITERS, n_col, CHUNKS)),
@@ -273,7 +309,7 @@
         compiler_params=pltpu.CompilerParams(
             collective_id=0, has_side_effects=True, vmem_limit_bytes=56 * 1024 * 1024
         ),
-    )(labels_prior, tiles, *plan(tile_rows, tile_cols, tile_count, group))
+    )(labels_prior, tiles, tile_rows.reshape(1, -1), tile_cols.reshape(1, -1), tile_count)
 
 
 def solution(mesh):

time: 56.2 us -> 41.2 us (0.73)
  Pallas kernels: 49.6 us -> 38.8 us
  other arithmetic: 4.14 us -> 0 us
    pallas_call x1, Pallas kernels: 49.6 us -> 38.8 us  [local(): pl.pallas_call(functools.partial(kernel, n_row, n_col), out_shape=jax.Sha...]
    reduce_sum x3 -> x0, other arithmetic: 1.76 us -> none  [the longest x1 1.45 us: plan(): jnp.sum(jnp.where(rank[:, None] + 1 == ids[None, :], row[:, None] + 1, 0)...]
    convert_element_type x2 -> x0, other arithmetic: 1.12 us -> none  [the longest x1 0.58 us: plan(): keep = (here == before).astype(jnp.int32)]
    add x3 -> x0, other arithmetic: 0.69 us -> none  [the longest x1 0.68 us: plan(): here = jnp.sum(jnp.where(hit, row[:, None] + 1, 0), axis=0)]
    max x1 -> x0, other arithmetic: 0.56 us -> none  [plan(): last = jnp.maximum(stop - 1, 0)]
where the time goes in v2:
time: 41.2 us; the launch traced here: 41 us
  Pallas kernels  38.8 us (94%)
  local copies, waits for them, and re-layouts  1.57 us (4%)
  between operations  0.66 us (2%)
    pallas_call x1, Pallas kernels, local(): pl.pallas_call(functools.partial(kernel, n_row, n_col), out_shape=jax.Sha...  38.8 us
    unnamed x1, local copies, waits for them, and re-layouts  1.57 us

profile of v2, /device:TPU:0, one launch (start us, length us, event | category | flops | bytes accessed | tf_op | source)
XLA Modules:
  0.0 41.0 jit_solution(4623862413871678199)
XLA Ops:
  0.7 38.8 %shard_map.55 = f32[16,2048]{1,0:T(8,128)} custom-call(f32[16,2048]{1,0:T(8,128)} %prior_ref.1, bf16[224,128,128]{2,1,0:T(8,128)(2,1)} %tiles_hbm.1, s32[1,224]{1,0:T(1,128)} %bitcast.2, s32[1,224]{1,0:T(1,128)} %bitcast.3, s32[1]{0:T(128)S(6)} %copy.7.count_ref), custom_call_target="tpu_custom_call" | custom-call | tf_op jit(solution)/shard_map/pallas_call | solution.py:280
  39.4 1.6 %copy.8 = f32[16,2048]{1,0:T(8,128)} copy(f32[16,2048]{1,0:T(8,128)} %shard_map.55) | data formatting | bytes 262144

commit v3 on v2

--- a/solution.py
+++ b/solution.py
@@ -12,7 +12,7 @@
 LEVELS = 65535.0
 CHUNKS = 2
 LOADS = 7
-UNROLL = 28
+UNROLL = 56
 
 
 def plan(rows, cols, count, table_ref, group_blocks):
@@ -49,11 +49,11 @@
 
 def kernel(
     n_row, n_col,
-    prior_ref, tiles_hbm, slot_rows_ref, slot_cols_ref, count_ref,
+    prior_hbm, tiles_hbm, slot_rows_ref, slot_cols_ref, count_ref,
     out_ref,
-    tiles_ref, ag0_ref, ag1_ref, run_ref, rows_ref, inv_ref, rows_in_ref, code_ref, code_in_ref,
+    prior_ref, tiles_ref, ag0_ref, ag1_ref, run_ref, rows_ref, inv_ref, rows_in_ref, code_ref, code_in_ref,
     cur_ref, scale_ref, table_ref, plan_ref, slot_sum_ref,
-    load_sem, plan_sem, ag_send, ag_recv, rs_send, rs_recv, row_send, row_recv,
+    prior_sem, load_sem, plan_sem, ag_send, ag_recv, rs_send, rs_recv, row_send, row_recv,
 ):
     labels, piece = prior_ref.shape
     slots, tile, _ = tiles_ref.shape
@@ -70,14 +70,8 @@
     def at(row, col):
         return {"row": row, "col": col}
 
-    loads = []
-    step = slots // LOADS
-    for n in range(LOADS):
-        window = pl.ds(n * step, step)
-        loads.append(
-            pltpu.make_async_copy(tiles_hbm.at[window], tiles_ref.at[window], load_sem.at[n])
-        )
-        loads[-1].start()
+    prior_copy = pltpu.make_async_copy(prior_hbm, prior_ref, prior_sem)
+    prior_copy.start()
 
     barrier = pltpu.get_barrier_semaphore()
     z_to = [None] + [((my_z + d) % n_z) * 2 + my_core for d in range(1, n_z)]
@@ -89,6 +83,15 @@
     pl.semaphore_signal(barrier, inc=1, device_id=at(partner, my_col))
     for d in range(1, n_col):
         pl.semaphore_signal(barrier, inc=1, device_id=at(my_row, c_to[d]))
+
+    loads = []
+    step = slots // LOADS
+    for n in range(LOADS):
+        window = pl.ds(n * step, step)
+        loads.append(
+            pltpu.make_async_copy(tiles_hbm.at[window], tiles_ref.at[window], load_sem.at[n])
+        )
+        loads[-1].start()
 
     def gather_copy(it, src_row, c, slot, to_row):
         window = pl.ds(src_row * own + c * part, part)
@@ -131,7 +134,8 @@
         ag0_ref[my_row * own + b] = value.astype(jnp.bfloat16)
         return carry
 
-    lax.fori_loop(0, own, round_prior, 0)
+    prior_copy.wait()
+    lax.fori_loop(0, own, round_prior, 0, unroll=True)
     pl.semaphore_wait(barrier, n_z + n_col - 1)
     sent = []
     for c in range(CHUNKS):
@@ -139,7 +143,7 @@
 
     def product(left, right):
         return lax.dot_general(
-            left, right, (((1,), (1,)), ((), ())), preferred_element_type=jnp.float32
+            left, right, (((1,), (0,)), ((), ())), preferred_element_type=jnp.float32
         )
 
     hot = plan(slot_rows_ref[...], slot_cols_ref[...], count_ref[0], table_ref, n_col * own)
@@ -155,7 +159,7 @@
             ],
             axis=0,
         )
-        both = product(left, jnp.concatenate([tiles_ref[n] for n in slot_pair], axis=1))
+        both = product(left, jnp.concatenate([tiles_ref[n] for n in slot_pair], axis=0))
         return both[:labels], both[labels:]
 
     ones = jnp.ones((labels, tile), jnp.bfloat16)
@@ -164,6 +168,8 @@
 
         def sum_pair(m, carry):
             k = n * step + 2 * m
+            for turned in (k, k + 1):
+                tiles_ref[turned] = tiles_ref[turned].T
             for i, value in enumerate(pair((ones, ones), (k, k + 1))):
                 slot_sum_ref[pl.ds(k + i, 1), :] = value[0:1]
             return carry
@@ -279,10 +285,11 @@
     vmem = pl.BlockSpec(memory_space=pltpu.VMEM)
     return pl.pallas_call(
         functools.partial(kernel, n_row, n_col),
-        out_shape=jax.ShapeDtypeStruct((labels, piece), jnp.float32),
-        in_specs=[vmem, pl.BlockSpec(memory_space=pl.ANY), vmem, vmem, smem],
+        out_shape=pltpu.VMEM((labels, piece), jnp.float32),
+        in_specs=[pl.BlockSpec(memory_space=pl.ANY)] * 2 + [vmem, vmem, smem],
         out_specs=vmem,
         scratch_shapes=[
+            pltpu.VMEM((labels, piece), jnp.float32),
             pltpu.VMEM((slots, tile, tile), jnp.bfloat16),
             pltpu.VMEM((n_row * own, labels, tile), jnp.bfloat16),
             pltpu.VMEM((n_row * own, labels, tile), jnp.bfloat16),
@@ -297,6 +304,7 @@
             pltpu.VMEM((8, width), jnp.int32),
             pltpu.SMEM((8, width), jnp.int32),
             pltpu.VMEM((slots, tile), jnp.float32),
+            pltpu.SemaphoreType.DMA(()),
             pltpu.SemaphoreType.DMA((LOADS,)),
             pltpu.SemaphoreType.DMA(()),
             pltpu.SemaphoreType.DMA((ITERS, 2 * n_z, CHUNKS)),

time: 41.2 us -> 36.7 us (0.89)
  Pallas kernels: 38.8 us -> 35.2 us
  local copies, waits for them, and re-layouts: 1.57 us -> 0.66 us
    pallas_call x1, Pallas kernels: 38.8 us -> 35.2 us  [local(): pl.pallas_call(functools.partial(kernel, n_row, n_col), out_shape=pltpu.V...]
    unnamed x1, local copies, waits for them, and re-layouts: 1.57 us -> 0.66 us
where the time goes in v3:
time: 36.7 us; the launch traced here: 36.5 us
  Pallas kernels  35.2 us (96%)
  local copies, waits for them, and re-layouts  0.66 us (2%)
  between operations  0.66 us (2%)
    pallas_call x1, Pallas kernels, local(): pl.pallas_call(functools.partial(kernel, n_row, n_col), out_shape=pltpu.V...  35.2 us

profile of v3, /device:TPU:0, one launch (start us, length us, event | category | flops | bytes accessed | tf_op | source)
XLA Modules:
  0.0 36.5 jit_solution(14852196735426305141)
XLA Ops:
  0.7 35.2 %shard_map.55 = f32[16,2048]{1,0:T(8,128)S(1)} custom-call(f32[16,2048]{1,0:T(8,128)} %prior_hbm.1, bf16[224,128,128]{2,1,0:T(8,128)(2,1)} %tiles_hbm.1, s32[1,224]{1,0:T(1,128)} %bitcast.2, s32[1,224]{1,0:T(1,128)} %bitcast.3, s32[1]{0:T(128)S(6)} %copy.8.count_ref), custom_call_target="tpu_custom_call" | custom-call | tf_op jit(solution)/shard_map/pallas_call | solution.py:286
  35.9 0.7 %copy.7 = f32[16,2048]{1,0:T(8,128)} copy(f32[16,2048]{1,0:T(8,128)S(1)} %shard_map.55) | data formatting | bytes 262144

commit v4 on v3

--- a/solution.py
+++ b/solution.py
@@ -104,10 +104,9 @@
         )
 
     def gather_start(it, c):
-        copies = []
-        for d in list(range(n_z - 1, 0, -1)):
+        copies = [gather_copy(it, my_row, c, n_z, partner)]
+        for d in range(1, n_z):
             copies.append(gather_copy(it, my_row, c, d, z_to[d]))
-        copies.append(gather_copy(it, my_row, c, n_z, partner))
         for copy in copies:
             copy.start()
         return copies

time: 36.7 us -> 35.6 us (0.970)
  Pallas kernels: 35.2 us -> 34.1 us
    pallas_call x1, Pallas kernels: 35.2 us -> 34.1 us  [local(): pl.pallas_call(functools.partial(kernel, n_row, n_col), out_shape=pltpu.V...]
where the time goes in v4:
time: 35.6 us; the launch traced here: 35.4 us
  Pallas kernels  34.1 us (96%)
  local copies, waits for them, and re-layouts  0.66 us (2%)
  between operations  0.66 us (2%)
    pallas_call x1, Pallas kernels, local(): pl.pallas_call(functools.partial(kernel, n_row, n_col), out_shape=pltpu.V...  34.1 us

profile of v4, /device:TPU:0, one launch (start us, length us, event | category | flops | bytes accessed | tf_op | source)
XLA Modules:
  0.0 35.4 jit_solution(14365209903354255104)
XLA Ops:
  0.7 34.1 %shard_map.55 = f32[16,2048]{1,0:T(8,128)S(1)} custom-call(f32[16,2048]{1,0:T(8,128)} %prior_hbm.1, bf16[224,128,128]{2,1,0:T(8,128)(2,1)} %tiles_hbm.1, s32[1,224]{1,0:T(1,128)} %bitcast.2, s32[1,224]{1,0:T(1,128)} %bitcast.3, s32[1]{0:T(128)S(6)} %copy.8.count_ref), custom_call_target="tpu_custom_call" | custom-call | tf_op jit(solution)/shard_map/pallas_call | solution.py:285
  34.7 0.7 %copy.7 = f32[16,2048]{1,0:T(8,128)} copy(f32[16,2048]{1,0:T(8,128)S(1)} %shard_map.55) | data formatting | bytes 262144
